TPU v7x, 128 devices: a whole 4x4x4 slice. The times are simulated.
128 devices in a mesh: ctx: 16 (over z_lo, y, core), ulys: 8 (over z_hi, x).
Axes of the slice: x: 4, y: 4, z: 4 (z_hi: 2, z_lo: 2; z = z_hi * 2 + z_lo), core: 2. Of those that a mesh axis runs over, the one named last changes fastest.
Arguments:
- queries: bfloat16 [32768, 2048], P(('ctx', 'ulys')), may hold values from -32 to 32
- keys: bfloat16 [32768, 2048], P(('ctx', 'ulys')), may hold values from -32 to 32
- values: bfloat16 [32768, 2048], P(('ctx', 'ulys')), may hold values from -6 to 6
- rand_blocks: int32 [512, 3], replicated, may hold values from 0 to 511, as said below
- out_weight: bfloat16 [2048, 4096], replicated, may hold values from -0.125 to 0.125
Outputs:
- output: bfloat16 [32768, 4096], P(('ctx', 'ulys'))
Inputs may be any that keep to these rules, and one draw needn't show every extreme that they name: `rand_blocks`: for the query blocks of one context group (rows 32 * c to 32 * c + 31), at most 12 of their random entries name blocks of any one group (blocks 32 * e to 32 * e + 31); every group's query blocks reach 12 for some group e.
All inputs are finite; a program needn't handle non-finite values.
Results may differ from a plain program's by a relative error of at most 0.0057.
Values may be sent and summed in bfloat16 or wider, within the bound.
A program may use at most 192 MiB of HBM per device.

v0:
```python
import jax
import jax.numpy as jnp
from jax import lax
from jax.sharding import PartitionSpec as P

DH = 128
BLK = 64
GLOB = 2
RAND = 3


def with_halo(block, sides, width):
    for axis, dim in sides:
        count = lax.axis_size(axis)
        forward = [(i, i + 1) for i in range(count - 1)]
        forward.append((count - 1, 0))
        backward = [(target, source) for source, target in forward]
        low = lax.ppermute(
            lax.slice_in_dim(block, block.shape[dim] - width, None, axis=dim), axis, forward
        )
        high = lax.ppermute(lax.slice_in_dim(block, 0, width, axis=dim), axis, backward)
        block = jnp.concatenate([low, block, high], axis=dim)
    return block


def spread(x, axis, root):
    mine = lax.axis_index(axis) == root
    return lax.psum(jnp.where(mine, x, jnp.zeros_like(x)), axis)


def pick_rows(held_rows, shard_rows, wanted):
    inside = (wanted >= 0) & (wanted < shard_rows.shape[1])
    taken_rows = jnp.take(shard_rows, jnp.clip(wanted, 0, shard_rows.shape[1] - 1), axis=1)
    return jnp.where(inside[None, :, :, :, None], taken_rows, held_rows)


def shards(queries, keys, values, rand_blocks, out_weight):
    q_heads, k_heads, v_heads = (
        lax.all_to_all(queries, "ulys", split_axis=1, concat_axis=0, tiled=True),
        lax.all_to_all(keys, "ulys", split_axis=1, concat_axis=0, tiled=True),
        lax.all_to_all(values, "ulys", split_axis=1, concat_axis=0, tiled=True),
    )
    span_len, lane_width = k_heads.shape
    heads_here = lane_width // DH
    group_id = lax.axis_index("ctx")
    blk_count = span_len // BLK
    paired = jnp.stack([k_heads, v_heads])
    padded = with_halo(paired, (("ctx", 1),), BLK)
    framed = padded.reshape(2, blk_count + 2, BLK, lane_width)
    leading = spread(paired[:, : GLOB * BLK], "ctx", 0)
    leading = jnp.broadcast_to(
        leading.reshape(2, 1, GLOB, BLK, lane_width), (2, blk_count, GLOB, BLK, lane_width)
    )
    my_rows = lax.dynamic_slice_in_dim(rand_blocks, group_id * blk_count, blk_count, 0)
    wanted = my_rows[:, :, None] * BLK + jnp.arange(BLK, dtype=jnp.int32)[None, None, :]
    blank_rows = jnp.zeros((2, blk_count, RAND, BLK, lane_width), paired.dtype)
    randoms = pick_rows(blank_rows, lax.all_gather(paired, "ctx", axis=1, tiled=True), wanted)
    listed = jnp.concatenate(
        [
            framed[:, :blk_count, None],
            framed[:, 1 : blk_count + 1, None],
            framed[:, 2:, None],
            leading,
            randoms,
        ],
        axis=2,
    )
    listed = listed.reshape(2, blk_count, -1, heads_here, DH)
    query_blk = q_heads.reshape(blk_count, BLK, heads_here, DH)
    scores = jnp.einsum(
        "bqhd,bkhd->bhqk", query_blk, listed[0], preferred_element_type=jnp.float32
    ) * DH ** (-0.5)
    peak_score = jnp.max(scores, axis=-1, keepdims=True)
    lifted = jnp.exp(scores - peak_score)
    weights = (lifted / jnp.sum(lifted, axis=-1, keepdims=True)).astype(jnp.bfloat16)
    attended = jnp.einsum("bhqk,bkhd->bqhd", weights, listed[1], preferred_element_type=jnp.float32)
    attended = attended.astype(jnp.bfloat16).reshape(span_len, lane_width)
    by_token = lax.all_to_all(attended, "ulys", split_axis=0, concat_axis=1, tiled=True)
    return jnp.dot(by_token, out_weight, preferred_element_type=jnp.float32).astype(jnp.bfloat16)


def solution(mesh):
    return jax.shard_map(
        shards,
        mesh=mesh,
        in_specs=(
            P(("ctx", "ulys"), None),
            P(("ctx", "ulys"), None),
            P(("ctx", "ulys"), None),
            P(),
            P(),
        ),
        out_specs=P(("ctx", "ulys"), None),
        check_vma=False,
    )
```

profile of v0, /device:TPU:1, one launch (start us, length us, event | category | flops | bytes accessed | tf_op | source)
XLA Modules:
  0.0 552.7 jit_solution(788128157725923596)
XLA Ops:
  6.5 2.3 copy.44
  8.8 8.2 %all-to-all-start = ((bf16[256,8,256]{0,2,1:T(8,128)(2,1)}), bf16[256,8,256]{0,2,1:T(8,128)(2,1)S(1)}, u32[]{:S(2)}, u32[]{:S(2)}) async-start(bf16[256,8,256]{0,2,1:T(8,128)(2,1)} %bitcast), calls=%async_computation | async-start | bytes 2097152 | tf_op jit(solution)/shard_map/all_to_all | solution.py:40
  17.0 2.2 copy.46
  19.2 15.1 %all-to-all-done = bf16[256,8,256]{0,2,1:T(8,128)(2,1)S(1)} async-done(((bf16[256,8,256]{0,2,1:T(8,128)(2,1)}), bf16[256,8,256]{0,2,1:T(8,128)(2,1)S(1)}, u32[]{:S(2)}, u32[]{:S(2)}) %all-to-all-start) | async-done | bytes 1048608 | tf_op jit(solution)/shard_map/all_to_all | solution.py:40
  34.3 3.6 all-to-all-start.1
  37.8 0.0 all-reduce.2.cloned.1.call-start
  37.9 0.5 copy.45
  38.4 16.7 %all-to-all-done.1 = bf16[256,8,256]{0,2,1:T(8,128)(2,1)S(1)} async-done(((bf16[256,8,256]{0,2,1:T(8,128)(2,1)}), bf16[256,8,256]{0,2,1:T(8,128)(2,1)S(1)}, u32[]{:S(2)}, u32[]{:S(2)}) %all-to-all-start.1) | async-done | bytes 1048608 | tf_op jit(solution)/shard_map/all_to_all | solution.py:41
  55.1 0.5 copy.47
  55.6 0.0 copy-start.1
  55.6 0.7 fusion.24
  56.3 0.0 all-reduce.2.cloned.1.call-update
  56.3 0.0 all-gather.2.cloned.1.call-start
  56.4 0.2 pad_maximum_fusion
  56.6 14.0 %copy.49 = bf16[2,2048,256]{2,0,1:T(2,128)(2,1)} copy(bf16[2,2048,256]{2,1,0:T(8,128)(2,1)S(1)} %pad_maximum_fusion) | data formatting | bytes 4194304 | tf_op jit(solution)/shard_map/stack | solution.py:47
  70.6 0.0 all-gather.2.cloned.1.call-update
  70.6 0.0 copy-done.1
  70.6 1.1 copy.77
  71.7 3.6 all-to-all-start.2
  75.2 0.8 dynamic-slice_multiply_fusion
  76.0 0.1 copy.48
  76.1 0.1 compare_select_fusion
  76.2 0.1 reshape.66
  76.3 0.2 compare_and_fusion
  76.5 2.1 collective-permute-start
  78.6 0.0 collective-permute-start.1
  78.6 13.9 %all-to-all-done.2 = bf16[256,8,256]{2,0,1:T(8,128)(2,1)S(1)} async-done(((bf16[256,8,256]{2,0,1:T(8,128)(2,1)}), bf16[256,8,256]{2,0,1:T(8,128)(2,1)S(1)}, u32[]{:S(2)}, u32[]{:S(2)}) %all-to-all-start.2) | async-done | bytes 1048608 | tf_op jit(solution)/shard_map/all_to_all | solution.py:39
  92.5 0.0 copy-start
  92.5 1.0 copy-done
  93.5 1.3 reshape.63
  94.9 0.0 collective-permute-done
  94.9 0.0 collective-permute-done.1
  94.9 0.1 pad_maximum_fusion.1
  95.0 1.5 fusion.15
  96.6 1.5 fusion.14
  98.1 1.5 fusion.13
  99.6 71.4 %all-reduce.2.cloned.1.call-done = bf16[2,2,64,256]{3,2,1,0:T(8,128)(2,1)} async-done(((bf16[2,2,64,256]{3,2,1,0:T(8,128)(2,1)}), bf16[2,2,64,256]{3,2,1,0:T(8,128)(2,1)}) %all-reduce.2.cloned.1.call-update) | async-done | bytes 131088 | tf_op jit(solution)/shard_map/psum | solution.py:28
  171.0 3.3 broadcast_dynamic-update-slice_fusion
  174.3 170.6 %all-gather.2.cloned.1.call-done = bf16[2,32768,256]{2,0,1:T(2,128)(2,1)} async-done(((bf16[2,2048,256]{2,0,1:T(2,128)(2,1)}), bf16[2,32768,256]{2,0,1:T(2,128)(2,1)}) %all-gather.2.cloned.1.call-update) | async-done | bytes 33554448 | tf_op jit(solution)/shard_map/all_gather | solution.py:57
  344.9 100.4 %gather_fusion = bf16[6144,2,256]{2,1,0:T(2,128)(2,1)} fusion(bf16[2,32768,256]{2,0,1:T(2,128)(2,1)} %all-gather.2.cloned.1.call-done, s32[6144]{0:T(1024)S(1)} %broadcast_clamp_fusion), kind=kCustom, calls=%fused_computation | custom fusion | bytes 12607488 | tf_op jit(solution)/shard_map/jit(_take)/gather | solution.py:33
  445.3 8.1 %bitcast_dynamic-update-slice_fusion = bf16[2,32,8,64,256]{4,3,2,1,0:T(8,128)(2,1)} fusion(bf16[2,32,8,64,256]{4,3,2,1,0:T(8,128)(2,1)} %broadcast_dynamic-update-slice_fusion, bf16[32,3,64,2,256]{4,3,2,1,0:T(2,128)(2,1)} %bitcast.66, pred[32,3,64]{2,1,0:T(4,128)(4,1)S(1)} %get-tuple-element.10, pred[32,3,64]{2,1,0:T(4,128)(4,1)S(1)} %get-tuple-element.9), kind=kLoop, calls=%fused_computation.12 | loop fusion | flops 6291456 | bytes 12595200 | tf_op jit(solution)/shard_map/concatenate | solution.py:58
  453.4 11.9 %fusion.31 = (bf16[1,32,8,64,256]{4,3,2,1,0:T(8,128)(2,1)}, bf16[1,32,8,64,256]{4,3,2,1,0:T(8,128)(2,1)}) fusion(bf16[2,32,8,64,256]{4,3,2,1,0:T(8,128)(2,1)} %bitcast_dynamic-update-slice_fusion), kind=kLoop, calls=%fused_computation.51 | loop fusion | bytes 33554432 | tf_op jit(solution)/shard_map/slice | solution.py:71
  465.3 12.6 %squeeze.7 = bf16[32,512,2,128]{3,2,1,0:T(2,128)(2,1)} reshape(bf16[1,32,8,64,256]{4,3,2,1,0:T(8,128)(2,1)} %get-tuple-element.5) | data formatting | bytes 16777216 | tf_op jit(solution)/shard_map/squeeze | solution.py:71
  477.8 6.4 %fusion.5 = f32[32,2,512,64]{2,3,1,0:T(8,128)S(1)} fusion(bf16[32,512,2,128]{3,2,1,0:T(2,128)(2,1)} %squeeze.7, bf16[32,64,2,128]{3,2,1,0:T(2,128)(2,1)S(1)} %reshape.63), kind=kOutput, calls=%fused_computation.8 | convolution fusion | flops 536870912 | bytes 17825792 | tf_op jit(solution)/shard_map/bqhd,bkhd->bhqk/dot_general | solution.py:70
  484.3 4.2 fusion.32
  488.5 12.5 %squeeze.6 = bf16[32,512,2,128]{3,2,1,0:T(2,128)(2,1)} reshape(bf16[1,32,8,64,256]{4,3,2,1,0:T(8,128)(2,1)} %get-tuple-element.6) | data formatting | bytes 16777216 | tf_op jit(solution)/shard_map/squeeze | solution.py:76
  501.0 7.6 %fusion.19 = bf16[32,64,2,128]{3,1,2,0:T(8,128)(2,1)S(1)} fusion(bf16[32,512,2,128]{3,2,1,0:T(2,128)(2,1)} %squeeze.6, f32[32,2,64,512]{3,2,1,0:T(8,128)} %get-tuple-element.12, f32[32,2,64]{2,1,0:T(2,128)S(1)} %get-tuple-element.11), kind=kOutput, calls=%fused_computation.34 | convolution fusion | flops 541589504 | bytes 17842176 | tf_op jit(solution)/shard_map/bhqk,bkhd->bqhd/dot_general | solution.py:76
  508.6 1.1 copy.58
  509.7 0.7 all_to_all.59
  510.4 23.4 %all_to_all.67 = bf16[8,256,256]{2,1,0:T(8,128)(2,1)S(1)} all-to-all(bf16[8,256,256]{2,1,0:T(8,128)(2,1)S(1)} %all_to_all.59), channel_id=1, replica_groups=mesh['ctx'=16,'ulys'=8] {'ulys'}, dimensions={0} | all-to-all | bytes 2097152 | tf_op jit(solution)/shard_map/all_to_all | solution.py:78
  533.8 0.5 copy.59
  534.4 11.5 %convolution_convert_fusion = bf16[256,4096]{1,0:T(8,128)(2,1)} fusion(bf16[256,2048]{0,1:T(8,128)(2,1)S(1)} %bitcast.67, bf16[2048,4096]{1,0:T(8,128)(2,1)} %param.9), kind=kOutput, calls=%fused_computation.15 | convolution fusion | flops 4296015872 | bytes 19922944 | tf_op jit(solution)/shard_map/dot_general | solution.py:79
  (2 shorter events, 0.0 us)
Async XLA Ops:
  8.8 25.5 %all-to-all-start = ((bf16[256,8,256]{0,2,1:T(8,128)(2,1)}), bf16[256,8,256]{0,2,1:T(8,128)(2,1)S(1)}, u32[]{:S(2)}, u32[]{:S(2)}) async-start(bf16[256,8,256]{0,2,1:T(8,128)(2,1)} %bitcast), calls=%async_computation | async-start | bytes 2097152 | tf_op jit(solution)/shard_map/all_to_all | solution.py:40
  34.3 20.8 %all-to-all-start.1 = ((bf16[256,8,256]{0,2,1:T(8,128)(2,1)}), bf16[256,8,256]{0,2,1:T(8,128)(2,1)S(1)}, u32[]{:S(2)}, u32[]{:S(2)}) async-start(bf16[256,8,256]{0,2,1:T(8,128)(2,1)} %bitcast.3), calls=%async_computation.1 | async-start | bytes 2097152 | tf_op jit(solution)/shard_map/all_to_all | solution.py:41
  37.8 133.1 %all-reduce.2.cloned.1.call-start = ((), (), s32[]{:S(2)}) async-start(), calls=%async_computation.4 | async-start | bytes 262144 | tf_op jit(solution)/shard_map/psum | solution.py:28
  55.6 15.0 %copy-start.1 = (bf16[256,2048]{1,0:T(8,128)(2,1)S(1)}, bf16[256,2048]{1,0:T(8,128)(2,1)}, u32[]{:S(2)}) copy-start(bf16[256,2048]{1,0:T(8,128)(2,1)} %param.5) | copy-start | bytes 3145732
  56.3 288.5 %all-gather.2.cloned.1.call-start = ((), (), s32[]{:S(2)}) async-start(), calls=%async_computation.5 | async-start | bytes 35651584 | tf_op jit(solution)/shard_map/all_gather | solution.py:57
  71.7 20.8 %all-to-all-start.2 = ((bf16[256,8,256]{2,0,1:T(8,128)(2,1)}), bf16[256,8,256]{2,0,1:T(8,128)(2,1)S(1)}, u32[]{:S(2)}, u32[]{:S(2)}) async-start(bf16[256,8,256]{2,0,1:T(8,128)(2,1)} %bitcast.69), calls=%async_computation.2 | async-start | bytes 2097152 | tf_op jit(solution)/shard_map/all_to_all | solution.py:39
  76.5 18.4 %collective-permute-start = (bf16[2,64,256]{2,1,0:T(8,128)(2,1)S(1)}, bf16[2,64,256]{2,1,0:T(8,128)(2,1)S(1)}, u32[]{:S(2)}, u32[]{:S(2)}) collective-permute-start(bf16[2,64,256]{2,1,0:T(8,128)(2,1)S(1)} %get-tuple-element.7), channel_id=1, source_target_pairs={{0,8},{8,16},{16,24},{24,32},{32,40},{40,48},{48,56},{56,64},{64,7... | collective-permute-start | bytes 196616 | tf_op jit(solution)/shard_map/ppermute | solution.py:18
  78.6 16.3 %collective-permute-start.1 = (bf16[2,64,256]{2,1,0:T(8,128)(2,1)S(1)}, bf16[2,64,256]{2,1,0:T(8,128)(2,1)S(1)}, u32[]{:S(2)}, u32[]{:S(2)}) collective-permute-start(bf16[2,64,256]{2,1,0:T(8,128)(2,1)S(1)} %get-tuple-element.8), channel_id=1, source_target_pairs={{8,0},{16,8},{24,16},{32,24},{40,32},{48,40},{56,48},{64,56},{72,6... | collective-permute-start | bytes 196616 | tf_op jit(solution)/shard_map/ppermute | solution.py:21
  92.5 1.0 copy-start
Sparse Core Ops, SparseCore 0:
  56.5 114.4 all-reduce.1
  172.8 172.0 all-gather.1
where the time goes:
time: 555 us; the launch traced here: 553 us
  waiting for transfers between devices  288 us (52%)
  local copies, waits for them, and re-layouts  171 us (31%)
  matrix products  25.6 us (5%)
  blocking collectives  23.4 us (4%)
  starting transfers between devices  17.4 us (3%)
  other arithmetic  14.3 us (3%)
  between operations  13.6 us (2%)
    all_gather x1, waiting for transfers between devices, shards(): lax.all_gather(paired, 'ctx', axis=1, tiled=True)  171 us
    gather x1, local copies, waits for them, and re-layouts, pick_rows(): jnp.take(shard_rows, jnp.clip(wanted, 0, shard_rows.shape[1] - 1), axis=1)  100 us
    psum x1, waiting for transfers between devices, spread(): return lax.psum(jnp.where(mine, x, jnp.zeros_like(x)), axis)  71.4 us
    all_to_all x1, blocking collectives, shards(): lax.all_to_all(attended, 'ulys', split_axis=0, concat_axis=1, tiled=True)  23.4 us
    all_to_all x1, waiting for transfers between devices, shards(): lax.all_to_all(values, 'ulys', split_axis=1, concat_axis=0, tiled=True)  16.7 us
    all_to_all x1, waiting for transfers between devices, shards(): lax.all_to_all(keys, 'ulys', split_axis=1, concat_axis=0, tiled=True)  15.1 us
    another operation x1, local copies, waits for them, and re-layouts, shards(): paired = jnp.stack([k_heads, v_heads])  14 us
    all_to_all x1, waiting for transfers between devices, shards(): lax.all_to_all(queries, 'ulys', split_axis=1, concat_axis=0, tiled=True)  13.9 us
  transfers between devices with their start and end apart: 7, of which 5 were waited for; matrix products, arithmetic and copies ran while one was open for 5% of the time, Pallas kernels for 0%

commit v1 on v0

v1 whole, which is shorter than its diff:
```python
import functools

import jax
import jax.numpy as jnp
from jax import lax
from jax.experimental import pallas as pl
from jax.experimental.pallas import tpu as pltpu
from jax.sharding import PartitionSpec as P

H = 16
DH = 128
D = 4096
BLK = 64
NB = 512
TOKENS = 32768
SHARE = 256
MESH = pl.DeviceIdType.MESH
LAG = 2
LAG_FAR = 4
TILE_N = 512
EXP_SCALE = (DH ** -0.5) * 1.4426950408889634


def mesh_id(x, y, z, core):
    return ((lax.rem(z, 2) * 4 + y) * 2 + core, lax.div(z, 2) * 4 + x)


def token_share(x, y, z, core):
    ctx, ulys = mesh_id(x, y, z, core)
    return ctx * 8 + ulys


def kernel(rand, q_in, k_in, v_in, w_in, out,
           kv, qb, ob, att, wv, outv,
           own_sem, s1_send, s1_recv, q_recv, up_recv, dn_recv, far_recv,
           ring_send, sib_send, sib_recv, ret_send, ret_recv, w_sem, out_sem):
    ctx, ulys = lax.axis_index("ctx"), lax.axis_index("ulys")
    core = lax.rem(ctx, 2)
    y = lax.rem(lax.div(ctx, 2), 4)
    z = lax.div(ulys, 4) * 2 + lax.div(ctx, 8)
    x = lax.rem(ulys, 4)
    head = y * 4 + x
    z_up, z_dn, z_far = lax.rem(z + 1, 4), lax.rem(z + 3, 4), lax.rem(z + 2, 4)
    up, dn = mesh_id(x, y, z_up, core), mesh_id(x, y, z_dn, core)
    sib = mesh_id(x, y, z, 1 - core)

    def peer(k):
        return lax.rem(x + lax.rem(k, 4), 4), lax.rem(y + lax.div(k, 4), 4)

    def back(k):
        return lax.rem(x + 4 - lax.rem(k, 4), 4), lax.rem(y + 4 - lax.div(k, 4), 4)

    def lanes(h):
        return pl.ds(pl.multiple_of(h * DH, DH), DH)

    def rows(k, zz):
        px, py = peer(k)
        return pl.ds(token_share(px, py, zz, core) * 4, 4)

    my_rows = rows(0, z)
    w_copies = [
        pltpu.make_async_copy(w_in.at[pl.ds(i * 256, 256)], wv.at[pl.ds(i * 256, 256)], w_sem.at[i])
        for i in range(8)
    ]
    own = [
        pltpu.make_async_copy(k_in.at[:, :, lanes(head)], kv.at[0, my_rows], own_sem.at[0]),
        pltpu.make_async_copy(v_in.at[:, :, lanes(head)], kv.at[1, my_rows], own_sem.at[1]),
        pltpu.make_async_copy(q_in.at[:, lanes(head)], qb.at[pl.ds(0, SHARE)], own_sem.at[2]),
    ]
    for copy in own:
        copy.start()

    barrier = pltpu.get_barrier_semaphore()
    for device in (up, dn, sib):
        pl.semaphore_signal(barrier, inc=1, device_id=device, device_id_type=MESH)

    @pl.loop(1, 16)
    def _(k):
        px, py = back(k)
        pl.semaphore_signal(barrier, inc=1, device_id=mesh_id(px, py, z, core), device_id_type=MESH)

    pl.semaphore_wait(barrier, 18)

    def remote(src, dst, send, recv, device):
        return pltpu.make_async_remote_copy(
            src_ref=src, dst_ref=dst, send_sem=send, recv_sem=recv,
            device_id=device, device_id_type=MESH)

    @pl.loop(1, 16)
    def _(k):
        px, py = back(k)
        device = mesh_id(px, py, z, core)
        h = py * 4 + px
        remote(k_in.at[:, :, lanes(h)], kv.at[0, my_rows], s1_send.at[0], s1_recv.at[k], device).start()
        remote(v_in.at[:, :, lanes(h)], kv.at[1, my_rows], s1_send.at[1], s1_recv.at[k], device).start()

    @pl.loop(1, 16)
    def _(k):
        px, py = back(k)
        device = mesh_id(px, py, z, core)
        h = py * 4 + px
        slot = pl.ds(pl.multiple_of(k * SHARE, SHARE), SHARE)
        remote(q_in.at[:, lanes(h)], qb.at[slot], s1_send.at[2], q_recv, device).start()

    for copy in w_copies:
        copy.start()
    own[0].wait()
    own[1].wait()

    def wait_piece(piece, sem):
        pltpu.make_async_copy(piece, piece, sem).wait()

    def push(piece, send, recv, device):
        remote(piece, piece, send, recv, device).start()

    def spread(k):
        piece = kv.at[:, rows(k, z)]

        @pl.when(k > 0)
        def _():
            wait_piece(piece, s1_recv.at[k])
        push(piece, ring_send.at[0], up_recv.at[k], up)
        push(piece, ring_send.at[1], dn_recv.at[k], dn)
        push(piece, sib_send.at[0], sib_recv.at[0], sib)

    def relay(k):
        low = kv.at[:, rows(k, z_dn)]
        high = kv.at[:, rows(k, z_up)]
        wait_piece(low, up_recv.at[k])

        @pl.when(lax.rem(k, 2) == 0)
        def _():
            push(low, ring_send.at[2], far_recv.at[k], up)
        push(low, sib_send.at[1], sib_recv.at[1], sib)
        wait_piece(high, dn_recv.at[k])

        @pl.when(lax.rem(k, 2) == 1)
        def _():
            push(high, ring_send.at[3], far_recv.at[k], dn)
        push(high, sib_send.at[2], sib_recv.at[2], sib)

    def last(k):
        piece = kv.at[:, rows(k, z_far)]
        wait_piece(piece, far_recv.at[k])
        push(piece, sib_send.at[3], sib_recv.at[3], sib)

    @pl.loop(0, 16 + LAG_FAR)
    def _(i):
        @pl.when(i < 16)
        def _():
            spread(i)

        @pl.when((i >= LAG) & (i < 16 + LAG))
        def _():
            relay(i - LAG)

        @pl.when(i >= LAG_FAR)
        def _():
            last(i - LAG_FAR)

    own[2].wait()
    wait_piece(qb.at[pl.ds(0, 15 * SHARE)], q_recv)
    span = kv.at[:, pl.ds(0, 64)]
    for i in range(4):
        wait_piece(span, sib_recv.at[i])

    @pl.loop(0, 16)
    def _(k):
        px, py = peer(k)
        first = token_share(px, py, z, core) * 4
        outs = []
        for j in range(4):
            b = first + j
            picks = [
                lax.rem(b + NB - 1, NB), b, lax.rem(b + 1, NB), 0, 1,
                rand[b, 0], rand[b, 1], rand[b, 2],
            ]

            def listed(side):
                parts = []
                for pick in picks:
                    parts.append(kv[side, pick])
                return jnp.concatenate(parts, axis=0)

            q = qb[pl.ds(pl.multiple_of(k * SHARE + j * BLK, BLK), BLK), :]
            s = lax.dot_general(q, listed(0), (((1,), (1,)), ((), ())), preferred_element_type=jnp.float32)
            peak = jnp.max(s, axis=-1, keepdims=True)
            lifted = jnp.exp2((s - peak) * EXP_SCALE)
            total = jnp.sum(lifted, axis=-1, keepdims=True)
            weights = (lifted / total).astype(jnp.bfloat16)
            outs.append(jnp.dot(weights, listed(1), preferred_element_type=jnp.float32).astype(jnp.bfloat16))
        slot = pl.ds(pl.multiple_of(k * SHARE, SHARE), SHARE)
        ob[slot, :] = jnp.concatenate(outs, axis=0)

        @pl.when(k > 0)
        def _():
            remote(ob.at[slot], att.at[:, lanes(head)], ret_send, ret_recv, mesh_id(px, py, z, core)).start()

    keep = pltpu.make_async_copy(ob.at[pl.ds(0, SHARE)], att.at[:, lanes(head)], own_sem.at[0])
    keep.start()
    for copy in w_copies:
        copy.wait()
    keep.wait()
    fifteen = ob.at[pl.ds(0, 15 * SHARE)]
    wait_piece(fifteen, ret_recv)

    @pl.loop(0, D // TILE_N)
    def _(n):
        cols = pl.ds(pl.multiple_of(n * TILE_N, TILE_N), TILE_N)
        outv[:, cols] = jnp.dot(att[...], wv[:, cols], preferred_element_type=jnp.float32).astype(jnp.bfloat16)
        pltpu.make_async_copy(outv.at[:, cols], out.at[:, cols], out_sem).start()

    wait_piece(outv, out_sem)
    wait_piece(fifteen, ret_send)
    for i in range(3):
        wait_piece(fifteen, s1_send.at[i])
    for i in range(2):
        wait_piece(span, ring_send.at[i])
    half = kv.at[:, pl.ds(0, 32)]
    for i in range(2, 4):
        wait_piece(half, ring_send.at[i])
    for i in range(4):
        wait_piece(span, sib_send.at[i])


def shards(queries, keys, values, rand_blocks, out_weight):
    any_spec = pl.BlockSpec(memory_space=pl.ANY)
    dma = pltpu.SemaphoreType.DMA
    return pl.pallas_call(
        kernel,
        out_shape=jax.ShapeDtypeStruct((SHARE, D), jnp.bfloat16),
        in_specs=[pl.BlockSpec(memory_space=pltpu.SMEM)] + [any_spec] * 4,
        out_specs=any_spec,
        scratch_shapes=[
            pltpu.VMEM((2, NB, BLK, DH), jnp.bfloat16),
            pltpu.VMEM((16 * SHARE, DH), jnp.bfloat16),
            pltpu.VMEM((16 * SHARE, DH), jnp.bfloat16),
            pltpu.VMEM((SHARE, H * DH), jnp.bfloat16),
            pltpu.VMEM((H * DH, D), jnp.bfloat16),
            pltpu.VMEM((SHARE, D), jnp.bfloat16),
            dma((3,)), dma((3,)), dma((16,)), dma, dma((16,)), dma((16,)), dma((16,)),
            dma((4,)), dma((4,)), dma((4,)), dma, dma, dma((8,)), dma,
        ],
        compiler_params=pltpu.CompilerParams(
            collective_id=0, has_side_effects=True, vmem_limit_bytes=56 * 1024 * 1024),
    )(rand_blocks, queries, keys.reshape(4, BLK, H * DH), values.reshape(4, BLK, H * DH), out_weight)


def solution(mesh):
    return jax.shard_map(
        shards,
        mesh=mesh,
        in_specs=(
            P(("ctx", "ulys"), None),
            P(("ctx", "ulys"), None),
            P(("ctx", "ulys"), None),
            P(),
            P(),
        ),
        out_specs=P(("ctx", "ulys"), None),
        check_vma=False,
    )
```

time: 555 us -> 127 us (0.23)
  waiting for transfers between devices: 288 us -> 0 us
  local copies, waits for them, and re-layouts: 171 us -> 4.68 us
  Pallas kernels: 0 us -> 122 us
  matrix products: 25.6 us -> 0 us
  blocking collectives: 23.4 us -> 0 us
  starting transfers between devices: 17.4 us -> 0 us
  other arithmetic: 14.3 us -> 0 us
  between operations: 13.6 us -> 0.01 us
    all_gather x1 -> x0, waiting for transfers between devices: 171 us -> none  [shards(): lax.all_gather(paired, 'ctx', axis=1, tiled=True)]
    pallas_call x0 -> x1, Pallas kernels: none -> 122 us  [shards(): pl.pallas_call(kernel, out_shape=jax.ShapeDtypeStruct((SHARE, D), jnp.bfl...]
    gather x1 -> x0, local copies, waits for them, and re-layouts: 100 us -> none  [pick_rows(): jnp.take(shard_rows, jnp.clip(wanted, 0, shard_rows.shape[1] - 1), axis=1)]
    psum x1 -> x0, waiting for transfers between devices: 71.4 us -> none  [spread(): return lax.psum(jnp.where(mine, x, jnp.zeros_like(x)), axis)]
    all_to_all x3 -> x0, waiting for transfers between devices: 45.7 us -> none  [the longest x1 16.7 us: shards(): lax.all_to_all(values, 'ulys', split_axis=1, concat_axis=0, tiled=True)]
    dot_general x3 -> x0, matrix products: 25.6 us -> none  [the longest x1 11.5 us: shards(): jnp.dot(by_token, out_weight, preferred_element_type=jnp.float32)]
    squeeze x2 -> x0, local copies, waits for them, and re-layouts: 25.1 us -> none  [the longest x1 12.6 us: shards(): listed[0]]
    all_to_all x1 -> x0, blocking collectives: 23.4 us -> none  [shards(): lax.all_to_all(attended, 'ulys', split_axis=0, concat_axis=1, tiled=True)]
  transfers between devices with their start and end apart: 7 -> 0, of which waited for: 5 -> 0; matrix products, arithmetic and copies ran while one was open for 5% -> 0% of each run, Pallas kernels for 0% -> 0%
where the time goes in v1:
time: 127 us
  Pallas kernels  122 us (96%)
  local copies, waits for them, and re-layouts  4.68 us (4%)
    pallas_call x1, Pallas kernels, shards(): pl.pallas_call(kernel, out_shape=jax.ShapeDtypeStruct((SHARE, D), jnp.bfl...  122 us
    unnamed x2, local copies, waits for them, and re-layouts  4.68 us

profile of v1, /device:TPU:1, one launch (start us, length us, event | category | flops | bytes accessed | tf_op | source)
XLA Modules:
  0.0 126.7 jit_solution(2260209359996438999)
XLA Ops:
  0.0 1.5 %copy.6.rand = s32[512,3]{1,0:T(8,128)} copy(s32[512,3]{0,1:T(4,128)} %param.8) | data formatting | bytes 12288 | tf_op args[3]
  1.6 122.0 %shard_map.55 = bf16[256,4096]{1,0:T(8,128)(2,1)} custom-call(s32[512,3]{1,0:T(8,128)} %copy.6.rand, bf16[256,2048]{1,0:T(8,128)(2,1)} %q_in.1, bf16[4,64,2048]{2,1,0:T(8,128)(2,1)} %bitcast.2, bf16[4,64,2048]{2,1,0:T(8,128)(2,1)} %bitcast.3, bf16[2048,4096]{1,0:T(8,128)(2,1)} %w_in.1), custom_call_target="tpu_custom_call" | custom-call | tf_op jit(solution)/shard_map/pallas_call | solution.py:229
  123.6 3.1 %copy.8 = bf16[256,4096]{1,0:T(8,128)(2,1)} copy(bf16[256,4096]{1,0:T(8,128)(2,1)} %shard_map.55) | data formatting | bytes 4194304

commit v2 on v1

--- a/solution.py
+++ b/solution.py
@@ -18,6 +18,7 @@
 LAG = 2
 LAG_FAR = 4
 TILE_N = 512
+GANG = 2
 EXP_SCALE = (DH ** -0.5) * 1.4426950408889634
 
 
@@ -164,37 +165,46 @@
     for i in range(4):
         wait_piece(span, sib_recv.at[i])
 
-    @pl.loop(0, 16)
-    def _(k):
-        px, py = peer(k)
-        first = token_share(px, py, z, core) * 4
-        outs = []
-        for j in range(4):
-            b = first + j
-            picks = [
-                lax.rem(b + NB - 1, NB), b, lax.rem(b + 1, NB), 0, 1,
-                rand[b, 0], rand[b, 1], rand[b, 2],
-            ]
-
-            def listed(side):
-                parts = []
-                for pick in picks:
-                    parts.append(kv[side, pick])
-                return jnp.concatenate(parts, axis=0)
-
-            q = qb[pl.ds(pl.multiple_of(k * SHARE + j * BLK, BLK), BLK), :]
-            s = lax.dot_general(q, listed(0), (((1,), (1,)), ((), ())), preferred_element_type=jnp.float32)
-            peak = jnp.max(s, axis=-1, keepdims=True)
-            lifted = jnp.exp2((s - peak) * EXP_SCALE)
-            total = jnp.sum(lifted, axis=-1, keepdims=True)
-            weights = (lifted / total).astype(jnp.bfloat16)
-            outs.append(jnp.dot(weights, listed(1), preferred_element_type=jnp.float32).astype(jnp.bfloat16))
-        slot = pl.ds(pl.multiple_of(k * SHARE, SHARE), SHARE)
-        ob[slot, :] = jnp.concatenate(outs, axis=0)
-
-        @pl.when(k > 0)
-        def _():
-            remote(ob.at[slot], att.at[:, lanes(head)], ret_send, ret_recv, mesh_id(px, py, z, core)).start()
+    @pl.loop(0, 16 // GANG)
+    def _(g):
+        lists, queries = [], []
+        for i in range(GANG):
+            px, py = peer(g * GANG + i)
+            first = token_share(px, py, z, core) * 4
+            for j in range(4):
+                b = first + j
+                lists.append([
+                    lax.rem(b + NB - 1, NB), b, lax.rem(b + 1, NB), 0, 1,
+                    rand[0, b], rand[1, b], rand[2, b],
+                ])
+                start = pl.multiple_of(g * GANG * SHARE + (i * 4 + j) * BLK, BLK)
+                queries.append(qb[pl.ds(start, BLK), :])
+
+        def listed(side, picks):
+            return jnp.concatenate([kv[side, pick] for pick in picks], axis=0)
+
+        scores = [
+            lax.dot_general(q, listed(0, picks), (((1,), (1,)), ((), ())), preferred_element_type=jnp.float32)
+            for q, picks in zip(queries, lists)
+        ]
+        peaks = [jnp.max(s, axis=-1, keepdims=True) for s in scores]
+        lifted = [jnp.exp2((s - peak) * EXP_SCALE) for s, peak in zip(scores, peaks)]
+        scales = [1.0 / jnp.sum(e, axis=-1, keepdims=True) for e in lifted]
+        weights = [(e * scale).astype(jnp.bfloat16) for e, scale in zip(lifted, scales)]
+        outs = [
+            jnp.dot(w, listed(1, picks), preferred_element_type=jnp.float32).astype(jnp.bfloat16)
+            for w, picks in zip(weights, lists)
+        ]
+        start = pl.multiple_of(g * GANG * SHARE, GANG * SHARE)
+        ob[pl.ds(start, GANG * SHARE), :] = jnp.concatenate(outs, axis=0)
+        for i in range(GANG):
+            k = g * GANG + i
+            px, py = peer(k)
+            slot = pl.ds(pl.multiple_of(k * SHARE, SHARE), SHARE)
+
+            @pl.when(k > 0)
+            def _():
+                remote(ob.at[slot], att.at[:, lanes(head)], ret_send, ret_recv, mesh_id(px, py, z, core)).start()
 
     keep = pltpu.make_async_copy(ob.at[pl.ds(0, SHARE)], att.at[:, lanes(head)], own_sem.at[0])
     keep.start()
@@ -243,7 +253,7 @@
         ],
         compiler_params=pltpu.CompilerParams(
             collective_id=0, has_side_effects=True, vmem_limit_bytes=56 * 1024 * 1024),
-    )(rand_blocks, queries, keys.reshape(4, BLK, H * DH), values.reshape(4, BLK, H * DH), out_weight)
+    )(rand_blocks.T, queries, keys.reshape(4, BLK, H * DH), values.reshape(4, BLK, H * DH), out_weight)
 
 
 def solution(mesh):

time: 127 us -> 111 us (0.87)
  Pallas kernels: 122 us -> 107 us
  local copies, waits for them, and re-layouts: 4.68 us -> 3.13 us
    pallas_call x1, Pallas kernels: 122 us -> 107 us  [shards(): pl.pallas_call(kernel, out_shape=jax.ShapeDtypeStruct((SHARE, D), jnp.bfl...]
    unnamed x2 -> x1, local copies, waits for them, and re-layouts: 4.68 us -> 3.13 us
where the time goes in v2:
time: 111 us
  Pallas kernels  107 us (96%)
  local copies, waits for them, and re-layouts  3.13 us (3%)
    pallas_call x1, Pallas kernels, shards(): pl.pallas_call(kernel, out_shape=jax.ShapeDtypeStruct((SHARE, D), jnp.bfl...  107 us
    unnamed x1, local copies, waits for them, and re-layouts  3.13 us

profile of v2, /device:TPU:1, one launch (start us, length us, event | category | flops | bytes accessed | tf_op | source)
XLA Modules:
  0.0 110.6 jit_solution(1216242601166096803)
XLA Ops:
  0.0 107.4 %shard_map.55 = bf16[256,4096]{1,0:T(8,128)(2,1)} custom-call(s32[3,512]{1,0:T(4,128)} %bitcast.5, bf16[256,2048]{1,0:T(8,128)(2,1)} %q_in.1, bf16[4,64,2048]{2,1,0:T(8,128)(2,1)} %bitcast.3, bf16[4,64,2048]{2,1,0:T(8,128)(2,1)} %bitcast.4, bf16[2048,4096]{1,0:T(8,128)(2,1)} %w_in.1), custom_call_target="tpu_custom_call" | custom-call | tf_op jit(solution)/shard_map/pallas_call | solution.py:239
  107.5 3.1 %copy.7 = bf16[256,4096]{1,0:T(8,128)(2,1)} copy(bf16[256,4096]{1,0:T(8,128)(2,1)} %shard_map.55) | data formatting | bytes 4194304

commit v3 on v2

v3 whole, which is shorter than its diff:
```python
import functools

import jax
import jax.numpy as jnp
from jax import lax
from jax.experimental import pallas as pl
from jax.experimental.pallas import tpu as pltpu
from jax.sharding import PartitionSpec as P

H = 16
DH = 128
D = 4096
BLK = 64
NB = 512
TOKENS = 32768
SHARE = 256
MESH = pl.DeviceIdType.MESH
TILE_N = 512
LAG = 6
LAG_FAR = 12
WEIGH_AT = 28
FIRST_AT = 36
VMEM_MIB = 47
GANG = 2
EXP_SCALE = (DH ** -0.5) * 1.4426950408889634


def mesh_id(x, y, z, core):
    return ((lax.rem(z, 2) * 4 + y) * 2 + core, lax.div(z, 2) * 4 + x)


def token_share(x, y, z, core):
    ctx, ulys = mesh_id(x, y, z, core)
    return ctx * 8 + ulys


def kernel(rand, q_in, k_in, v_in, w_in, out,
           kb, vb0, vb1, qb, pb, va, vp, ob, att, wv, acc,
           own_sem, s1_send, k_recv, v_recv, q_recv, k_up, k_dn, k_far, v_up, v_dn, v_far,
           ring_send, sib_send, sib_recv, ret_send, ret_recv, w_sem, out_sem):
    ctx, ulys = lax.axis_index("ctx"), lax.axis_index("ulys")
    core = lax.rem(ctx, 2)
    y = lax.rem(lax.div(ctx, 2), 4)
    z = lax.div(ulys, 4) * 2 + lax.div(ctx, 8)
    x = lax.rem(ulys, 4)
    head = y * 4 + x
    z_up, z_dn, z_far = lax.rem(z + 1, 4), lax.rem(z + 3, 4), lax.rem(z + 2, 4)
    up, dn = mesh_id(x, y, z_up, core), mesh_id(x, y, z_dn, core)
    sib = mesh_id(x, y, z, 1 - core)
    vbs = (vb0, vb1)

    def peer(k):
        return lax.rem(x + lax.rem(k, 4), 4), lax.rem(y + lax.div(k, 4), 4)

    def back(k):
        return lax.rem(x + 4 - lax.rem(k, 4), 4), lax.rem(y + 4 - lax.div(k, 4), 4)

    def lanes(h):
        return pl.ds(pl.multiple_of(h * DH, DH), DH)

    def rows(k, zz):
        px, py = peer(k)
        return pl.ds(token_share(px, py, zz, core) * 4, 4)

    def rows_x(g, zz):
        return pl.ds(token_share(0, lax.rem(y + g, 4), zz, core) * 4, 16)

    def shares(k, count=1):
        return pl.ds(pl.multiple_of(k * SHARE, SHARE), count * SHARE)

    def packed(k, count=1):
        return pl.ds(pl.multiple_of(k * DH, DH), count * DH)

    my_rows = rows(0, z)
    own = [
        pltpu.make_async_copy(k_in.at[:, :, lanes(head)], kb.at[my_rows], own_sem.at[0]),
        pltpu.make_async_copy(v_in, va, own_sem.at[1]),
        pltpu.make_async_copy(q_in.at[:, lanes(head)], qb.at[shares(0)], own_sem.at[2]),
    ]
    for copy in own:
        copy.start()

    barrier = pltpu.get_barrier_semaphore()
    for device in (up, dn, sib):
        pl.semaphore_signal(barrier, inc=1, device_id=device, device_id_type=MESH)

    @pl.loop(1, 16)
    def _(k):
        px, py = back(k)
        pl.semaphore_signal(barrier, inc=1, device_id=mesh_id(px, py, z, core), device_id_type=MESH)

    pl.semaphore_wait(barrier, 18)

    def push(src, dst, send, recv, device):
        pltpu.make_async_remote_copy(
            src_ref=src, dst_ref=dst, send_sem=send, recv_sem=recv,
            device_id=device, device_id_type=MESH).start()

    def arrived(piece, sem):
        pltpu.make_async_copy(piece, piece, sem).wait()

    def send_on(side, piece, via, sem, device):
        push(piece, piece, ring_send.at[side, via], sem, device)

    def share_on(side, piece, plane):
        push(piece, piece, sib_send.at[side, plane], sib_recv.at[side, plane], sib)

    def relay(side, low, high, from_low, from_high, to_far, k):
        arrived(low, from_low)

        @pl.when(lax.rem(k, 2) == 0)
        def _():
            send_on(side, low, 2, to_far, up)
        share_on(side, low, 1)
        arrived(high, from_high)

        @pl.when(lax.rem(k, 2) == 1)
        def _():
            send_on(side, high, 3, to_far, dn)
        share_on(side, high, 2)

    def spread_k(k):
        piece = kb.at[rows(k, z)]
        send_on(0, piece, 0, k_up.at[k], up)
        send_on(0, piece, 1, k_dn.at[k], dn)
        share_on(0, piece, 0)

    def relay_k(k):
        relay(0, kb.at[rows(k, z_dn)], kb.at[rows(k, z_up)], k_up.at[k], k_dn.at[k], k_far.at[k], k)

    def last_k(k):
        piece = kb.at[rows(k, z_far)]
        arrived(piece, k_far.at[k])
        share_on(0, piece, 3)

    def spread_v(h, g):
        piece = vbs[h].at[rows_x(g, z)]
        arrived(piece, v_recv.at[h, g])
        send_on(1 + h, piece, 0, v_up.at[h, g], up)
        send_on(1 + h, piece, 1, v_dn.at[h, g], dn)
        share_on(1 + h, piece, 0)

    def relay_v(h, g):
        relay(1 + h, vbs[h].at[rows_x(g, z_dn)], vbs[h].at[rows_x(g, z_up)],
              v_up.at[h, g], v_dn.at[h, g], v_far.at[h, g], g)

    def last_v(h, g):
        piece = vbs[h].at[rows_x(g, z_far)]
        arrived(piece, v_far.at[h, g])
        share_on(1 + h, piece, 3)

    own[0].wait()
    spread_k(0)

    @pl.loop(1, 16)
    def _(k):
        px, py = back(k)
        push(k_in.at[:, :, lanes(py * 4 + px)], kb.at[my_rows], s1_send.at[0], k_recv.at[k], mesh_id(px, py, z, core))

    @pl.loop(1, 16)
    def _(k):
        px, py = back(k)
        push(q_in.at[:, lanes(py * 4 + px)], qb.at[shares(k)], s1_send.at[1], q_recv, mesh_id(px, py, z, core))

    own[1].wait()
    lane = lax.broadcasted_iota(jnp.int32, (1, DH), 1)
    low_half = lane < DH // 2

    def swap(a):
        return pltpu.roll(a, DH // 2, axis=1)

    @pl.loop(0, 16)
    def _(h):
        for blk in range(4):
            top = va[blk * BLK:blk * BLK + 32, lanes(h)].astype(jnp.float32)
            bottom = va[blk * BLK + 32:blk * BLK + 64, lanes(h)].astype(jnp.float32)
            vp[0, h, blk] = jnp.where(low_half, top, swap(bottom)).astype(jnp.bfloat16)
            vp[1, h, blk] = jnp.where(low_half, swap(top), bottom).astype(jnp.bfloat16)

    for h in range(2):
        pltpu.make_async_copy(vp.at[h, head], vbs[h].at[my_rows], v_recv.at[h, 0]).start()

        @pl.loop(1, 16)
        def _(k):
            px, py = back(k)
            push(vp.at[h, py * 4 + px], vbs[h].at[my_rows], s1_send.at[2 + h], v_recv.at[h, lax.div(k, 4)],
                 mesh_id(px, py, z, core))

    for h in range(2):
        @pl.loop(0, 16)
        def _(k):
            px, py = back(k)
            pltpu.make_async_copy(
                w_in.at[pl.ds(pl.multiple_of((py * 4 + px) * DH + h * 64, 64), 64)],
                wv.at[h, pl.ds(pl.multiple_of(k * 64, 64), 64)], w_sem.at[h]).start()
    own[2].wait()

    def blocks_of(g):
        found = []
        for i in range(GANG):
            px, py = peer(g * GANG + i)
            first = token_share(px, py, z, core) * 4
            for j in range(4):
                b = first + j
                found.append([
                    lax.rem(b + NB - 1, NB), b, lax.rem(b + 1, NB), 0, 1,
                    rand[0, b], rand[1, b], rand[2, b],
                ])
        return found

    def gang_rows(g, n):
        return pl.ds(pl.multiple_of(g * GANG * SHARE + n * BLK, BLK), BLK)

    def listed_keys(picks):
        blocks = [kb[pick] for pick in picks]
        return jnp.concatenate([b[0:32] for b in blocks] + [b[32:64] for b in blocks], axis=0)

    def weigh(g):
        scores = [
            lax.dot_general(qb[gang_rows(g, n), :], listed_keys(picks), (((1,), (1,)), ((), ())),
                            preferred_element_type=jnp.float32)
            for n, picks in enumerate(blocks_of(g))
        ]
        peaks = [jnp.max(s, axis=-1, keepdims=True) for s in scores]
        lifted = [jnp.exp2((s - peak) * EXP_SCALE) for s, peak in zip(scores, peaks)]
        scales = [1.0 / jnp.sum(e, axis=-1, keepdims=True) for e in lifted]
        for n, (e, scale) in enumerate(zip(lifted, scales)):
            pb[gang_rows(g, n), :] = (e * scale).astype(jnp.bfloat16)

    def attend(h, g):
        sums = []
        for n, picks in enumerate(blocks_of(g)):
            w = pb[gang_rows(g, n), :]
            w = jnp.concatenate([w[:, 0:256], w[:, 256:512]], axis=0)
            listed = jnp.concatenate([vbs[h][pick] for pick in picks], axis=0)
            sums.append(jnp.dot(w, listed, preferred_element_type=jnp.float32))
        outs = []
        for even, odd in zip(sums[0::2], sums[1::2]):
            outs.append(jnp.where(low_half, even[0:64] + swap(even[64:128]), swap(odd[0:64]) + odd[64:128]))
        ob[h, packed(g * GANG, GANG), :] = jnp.concatenate(outs, axis=0).astype(jnp.bfloat16)
        for i in range(GANG):
            k = g * GANG + i
            px, py = peer(k)

            @pl.when(k > 0)
            def _():
                push(ob.at[h, packed(k)], att.at[h, :, lanes(k)], ret_send.at[h], ret_recv.at[h], mesh_id(px, py, z, core))

            @pl.when(k == 0)
            def _():
                pltpu.make_async_copy(ob.at[h, packed(0)], att.at[h, :, pl.ds(0, DH)], ret_recv.at[h]).start()

    span = pl.ds(0, 64)
    half = pl.ds(0, 32)

    def at(i, begin, end):
        return (i >= begin) & (i < end)

    def at_even(i, begin):
        return (i >= begin) & (i < begin + 8) & (lax.rem(i - begin, 2) == 0)

    @pl.loop(1, 32 + LAG_FAR)
    def _(i):
        @pl.when(i < 16)
        def _():
            arrived(kb.at[rows(i, z)], k_recv.at[i])
            spread_k(i)

        for h in range(2):
            @pl.when(at_even(i, 16 + 8 * h))
            def _():
                spread_v(h, lax.div(i - 16 - 8 * h, 2))

        @pl.when(at(i, LAG, 16 + LAG))
        def _():
            relay_k(i - LAG)

        for h in range(2):
            @pl.when(at_even(i, 16 + 8 * h + LAG))
            def _():
                relay_v(h, lax.div(i - 16 - 8 * h - LAG, 2))

        @pl.when(at(i, LAG_FAR, 16 + LAG_FAR))
        def _():
            last_k(i - LAG_FAR)

        for h in range(2):
            @pl.when(at_even(i, 16 + 8 * h + LAG_FAR))
            def _():
                last_v(h, lax.div(i - 16 - 8 * h - LAG_FAR, 2))

        @pl.when(i == WEIGH_AT - 1)
        def _():
            arrived(qb.at[shares(0, 15)], q_recv)
            for plane in range(4):
                arrived(kb.at[span], sib_recv.at[0, plane])

        @pl.when(at(i, WEIGH_AT, WEIGH_AT + 16 // GANG))
        def _():
            weigh(i - WEIGH_AT)

        @pl.when(i == FIRST_AT - 1)
        def _():
            for plane in range(4):
                arrived(vb0.at[span], sib_recv.at[1, plane])

        @pl.when(at(i, FIRST_AT, FIRST_AT + 16 // GANG))
        def _():
            attend(0, i - FIRST_AT)

    for plane in range(4):
        arrived(vb1.at[span], sib_recv.at[2, plane])

    @pl.loop(0, 16 // GANG)
    def _(g):
        attend(1, g)

    def unpack(h):
        for pair in range(8):
            a = att[h, :, 2 * pair * DH:(2 * pair + 1) * DH].astype(jnp.float32)
            b = att[h, :, (2 * pair + 1) * DH:(2 * pair + 2) * DH].astype(jnp.float32)
            cols = slice(h * 1024 + pair * DH, h * 1024 + (pair + 1) * DH)
            va[0:128, cols] = jnp.where(low_half, a, swap(b)).astype(jnp.bfloat16)
            va[128:256, cols] = jnp.where(low_half, swap(a), b).astype(jnp.bfloat16)

    def tile(n):
        return pl.ds(pl.multiple_of(n * TILE_N, TILE_N), TILE_N)

    arrived(wv.at[0], w_sem.at[0])
    arrived(ob.at[0], ret_recv.at[0])
    unpack(0)

    @pl.loop(0, D // TILE_N)
    def _(n):
        acc[:, tile(n)] = jnp.dot(va[:, 0:1024], wv[0, :, tile(n)], preferred_element_type=jnp.float32)

    arrived(wv.at[1], w_sem.at[1])
    arrived(ob.at[1], ret_recv.at[1])
    unpack(1)

    @pl.loop(0, D // TILE_N)
    def _(n):
        total = acc[:, tile(n)] + jnp.dot(va[:, 1024:2048], wv[1, :, tile(n)], preferred_element_type=jnp.float32)
        total = total.astype(jnp.bfloat16)
        done = jnp.concatenate([total[0:64], total[128:192], total[64:128], total[192:256]], axis=0)
        pb[shares(n), :] = done
        pltpu.make_async_copy(pb.at[shares(n)], out.at[:, tile(n)], out_sem).start()

    for i in range(2):
        arrived(ob.at[0, packed(0, 15)], ret_send.at[i])
        arrived(qb.at[shares(0, 15)], s1_send.at[i])
        arrived(ob.at[0, packed(0, 15)], s1_send.at[2 + i])
    for side, buf in enumerate((kb, vb0, vb1)):
        for i in range(2):
            arrived(buf.at[span], ring_send.at[side, i])
        for i in range(2, 4):
            arrived(buf.at[half], ring_send.at[side, i])
        for i in range(4):
            arrived(buf.at[span], sib_send.at[side, i])
    arrived(pb.at[shares(0, D // TILE_N)], out_sem)


def shards(queries, keys, values, rand_blocks, out_weight):
    any_spec = pl.BlockSpec(memory_space=pl.ANY)
    dma = pltpu.SemaphoreType.DMA
    return pl.pallas_call(
        kernel,
        out_shape=jax.ShapeDtypeStruct((SHARE, D), jnp.bfloat16),
        in_specs=[pl.BlockSpec(memory_space=pltpu.SMEM)] + [any_spec] * 4,
        out_specs=any_spec,
        scratch_shapes=[
            pltpu.VMEM((NB, BLK, DH), jnp.bfloat16),
            pltpu.VMEM((NB, BLK // 2, DH), jnp.bfloat16),
            pltpu.VMEM((NB, BLK // 2, DH), jnp.bfloat16),
            pltpu.VMEM((16 * SHARE, DH), jnp.bfloat16),
            pltpu.VMEM((16 * SHARE, 8 * BLK), jnp.bfloat16),
            pltpu.VMEM((SHARE, H * DH), jnp.bfloat16),
            pltpu.VMEM((2, H, 4, BLK // 2, DH), jnp.bfloat16),
            pltpu.VMEM((2, 16 * SHARE // 2, DH), jnp.bfloat16),
            pltpu.VMEM((2, SHARE // 2, H * DH), jnp.bfloat16),
            pltpu.VMEM((2, H * DH // 2, D), jnp.bfloat16),
            pltpu.VMEM((SHARE, D), jnp.float32),
            dma((3,)), dma((4,)), dma((16,)), dma((2, 4)), dma,
            dma((16,)), dma((16,)), dma((16,)), dma((2, 4)), dma((2, 4)), dma((2, 4)),
            dma((3, 4)), dma((3, 4)), dma((3, 4)), dma((2,)), dma((2,)), dma((2,)), dma,
        ],
        compiler_params=pltpu.CompilerParams(
            collective_id=0, has_side_effects=True, vmem_limit_bytes=VMEM_MIB * 1024 * 1024),
    )(rand_blocks.T, queries, keys.reshape(4, BLK, H * DH), values, out_weight)


def solution(mesh):
    return jax.shard_map(
        shards,
        mesh=mesh,
        in_specs=(
            P(("ctx", "ulys"), None),
            P(("ctx", "ulys"), None),
            P(("ctx", "ulys"), None),
            P(),
            P(),
        ),
        out_specs=P(("ctx", "ulys"), None),
        check_vma=False,
    )
```

time: 111 us -> 106 us (0.955)
  Pallas kernels: 107 us -> 100 us
  local copies, waits for them, and re-layouts: 3.13 us -> 5.69 us
    pallas_call x1, Pallas kernels: 107 us -> 100 us  [shards(): pl.pallas_call(kernel, out_shape=jax.ShapeDtypeStruct((SHARE, D), jnp.bfl...]
    unnamed x1 -> x9, local copies, waits for them, and re-layouts: 3.13 us -> 5.69 us
where the time goes in v3:
time: 106 us
  Pallas kernels  100 us (94%)
  local copies, waits for them, and re-layouts  5.69 us (5%)
    pallas_call x1, Pallas kernels, shards(): pl.pallas_call(kernel, out_shape=jax.ShapeDtypeStruct((SHARE, D), jnp.bfl...  100 us
    unnamed x9, local copies, waits for them, and re-layouts  5.69 us

profile of v3, /device:TPU:1, one launch (start us, length us, event | category | flops | bytes accessed | tf_op | source)
XLA Modules:
  0.0 106.1 jit_solution(18065093806414964762)
XLA Ops:
  0.0 0.0 copy-start
  0.0 1.2 %copy-done = bf16[256,2048]{1,0:T(8,128)(2,1)S(1)} copy-done((bf16[256,2048]{1,0:T(8,128)(2,1)S(1)}, bf16[256,2048]{1,0:T(8,128)(2,1)}, u32[]{:S(2)}) %copy-start) | copy-done | bytes 1048600
  1.2 0.0 copy-start.1
  1.2 1.2 %copy-done.1 = bf16[256,2048]{1,0:T(8,128)(2,1)S(1)} copy-done((bf16[256,2048]{1,0:T(8,128)(2,1)S(1)}, bf16[256,2048]{1,0:T(8,128)(2,1)}, u32[]{:S(2)}) %copy-start.1) | copy-done | bytes 1048600
  2.5 0.0 copy-start.2
  2.5 1.2 %copy-done.2 = bf16[256,2048]{1,0:T(8,128)(2,1)S(1)} copy-done((bf16[256,2048]{1,0:T(8,128)(2,1)S(1)}, bf16[256,2048]{1,0:T(8,128)(2,1)}, u32[]{:S(2)}) %copy-start.2) | copy-done | bytes 1048600
  3.7 0.0 copy-start.3
  3.7 0.7 copy-done.3
  4.4 100.4 %shard_map.55 = bf16[256,4096]{1,0:T(8,128)(2,1)S(1)} custom-call(s32[3,512]{1,0:T(4,128)S(1)} %bitcast.3, bf16[256,2048]{1,0:T(8,128)(2,1)S(1)} %copy-done, bf16[4,64,2048]{2,1,0:T(8,128)(2,1)S(1)} %bitcast.2, bf16[256,2048]{1,0:T(8,128)(2,1)S(1)} %copy-done.2, bf16[2048,4096]{1,0:T(8,128)(2,1)} %w_in.1), custom_call_target="tpu_custom_call" | custom-call | tf_op jit(solution)/shard_map/pallas_call | solution.py:366
  104.8 1.3 %copy.7 = bf16[256,4096]{1,0:T(8,128)(2,1)} copy(bf16[256,4096]{1,0:T(8,128)(2,1)S(1)} %shard_map.55) | data formatting | bytes 4194304
Async XLA Ops:
  0.0 1.2 %copy-start = (bf16[256,2048]{1,0:T(8,128)(2,1)S(1)}, bf16[256,2048]{1,0:T(8,128)(2,1)}, u32[]{:S(2)}) copy-start(bf16[256,2048]{1,0:T(8,128)(2,1)} %q_in.1) | copy-start | bytes 3145732
  1.2 1.2 %copy-start.1 = (bf16[256,2048]{1,0:T(8,128)(2,1)S(1)}, bf16[256,2048]{1,0:T(8,128)(2,1)}, u32[]{:S(2)}) copy-start(bf16[256,2048]{1,0:T(8,128)(2,1)} %param.6) | copy-start | bytes 3145732
  2.5 1.2 %copy-start.2 = (bf16[256,2048]{1,0:T(8,128)(2,1)S(1)}, bf16[256,2048]{1,0:T(8,128)(2,1)}, u32[]{:S(2)}) copy-start(bf16[256,2048]{1,0:T(8,128)(2,1)} %v_in.1) | copy-start | bytes 3145732
  3.7 0.7 copy-start.3

commit v4 on v3

--- a/solution.py
+++ b/solution.py
@@ -18,8 +18,15 @@
 TILE_N = 512
 LAG = 6
 LAG_FAR = 12
+V_AT = (16, 26)
+V_LAG = 4
+V_FAR = 8
+Q_AT = 4
+PACK_AT = 6
+W_AT = 10
 WEIGH_AT = 28
-FIRST_AT = 36
+FIRST_AT = 32
+STOP = 42
 VMEM_MIB = 47
 GANG = 2
 EXP_SCALE = (DH ** -0.5) * 1.4426950408889634
@@ -157,43 +164,46 @@
         px, py = back(k)
         push(k_in.at[:, :, lanes(py * 4 + px)], kb.at[my_rows], s1_send.at[0], k_recv.at[k], mesh_id(px, py, z, core))
 
-    @pl.loop(1, 16)
-    def _(k):
-        px, py = back(k)
-        push(q_in.at[:, lanes(py * 4 + px)], qb.at[shares(k)], s1_send.at[1], q_recv, mesh_id(px, py, z, core))
-
-    own[1].wait()
-    lane = lax.broadcasted_iota(jnp.int32, (1, DH), 1)
-    low_half = lane < DH // 2
-
-    def swap(a):
-        return pltpu.roll(a, DH // 2, axis=1)
-
-    @pl.loop(0, 16)
-    def _(h):
-        for blk in range(4):
-            top = va[blk * BLK:blk * BLK + 32, lanes(h)].astype(jnp.float32)
-            bottom = va[blk * BLK + 32:blk * BLK + 64, lanes(h)].astype(jnp.float32)
-            vp[0, h, blk] = jnp.where(low_half, top, swap(bottom)).astype(jnp.bfloat16)
-            vp[1, h, blk] = jnp.where(low_half, swap(top), bottom).astype(jnp.bfloat16)
-
-    for h in range(2):
-        pltpu.make_async_copy(vp.at[h, head], vbs[h].at[my_rows], v_recv.at[h, 0]).start()
-
+    def send_queries():
         @pl.loop(1, 16)
         def _(k):
             px, py = back(k)
-            push(vp.at[h, py * 4 + px], vbs[h].at[my_rows], s1_send.at[2 + h], v_recv.at[h, lax.div(k, 4)],
-                 mesh_id(px, py, z, core))
-
-    for h in range(2):
+            push(q_in.at[:, lanes(py * 4 + px)], qb.at[shares(k)], s1_send.at[1], q_recv, mesh_id(px, py, z, core))
+
+    lane = lax.broadcasted_iota(jnp.int32, (1, DH), 1)
+    low_half = lane < DH // 2
+
+    def swap(a):
+        return pltpu.roll(a, DH // 2, axis=1)
+
+    def send_values():
+        own[1].wait()
+
         @pl.loop(0, 16)
-        def _(k):
-            px, py = back(k)
-            pltpu.make_async_copy(
-                w_in.at[pl.ds(pl.multiple_of((py * 4 + px) * DH + h * 64, 64), 64)],
-                wv.at[h, pl.ds(pl.multiple_of(k * 64, 64), 64)], w_sem.at[h]).start()
-    own[2].wait()
+        def _(h):
+            for blk in range(4):
+                top = va[blk * BLK:blk * BLK + 32, lanes(h)].astype(jnp.float32)
+                bottom = va[blk * BLK + 32:blk * BLK + 64, lanes(h)].astype(jnp.float32)
+                vp[0, h, blk] = jnp.where(low_half, top, swap(bottom)).astype(jnp.bfloat16)
+                vp[1, h, blk] = jnp.where(low_half, swap(top), bottom).astype(jnp.bfloat16)
+
+        for h in range(2):
+            pltpu.make_async_copy(vp.at[h, head], vbs[h].at[my_rows], v_recv.at[h, 0]).start()
+
+            @pl.loop(1, 16)
+            def _(k):
+                px, py = back(k)
+                push(vp.at[h, py * 4 + px], vbs[h].at[my_rows], s1_send.at[2 + h], v_recv.at[h, lax.div(k, 4)],
+                     mesh_id(px, py, z, core))
+
+    def load_weight():
+        for h in range(2):
+            @pl.loop(0, 16)
+            def _(k):
+                px, py = back(k)
+                pltpu.make_async_copy(
+                    w_in.at[pl.ds(pl.multiple_of((py * 4 + px) * DH + h * 64, 64), 64)],
+                    wv.at[h, pl.ds(pl.multiple_of(k * 64, 64), 64)], w_sem.at[h]).start()
 
     def blocks_of(g):
         found = []
@@ -259,38 +269,51 @@
     def at_even(i, begin):
         return (i >= begin) & (i < begin + 8) & (lax.rem(i - begin, 2) == 0)
 
-    @pl.loop(1, 32 + LAG_FAR)
+    @pl.loop(1, STOP)
     def _(i):
         @pl.when(i < 16)
         def _():
             arrived(kb.at[rows(i, z)], k_recv.at[i])
             spread_k(i)
 
+        @pl.when(i == Q_AT)
+        def _():
+            send_queries()
+
+        @pl.when(i == PACK_AT)
+        def _():
+            send_values()
+
+        @pl.when(i == W_AT)
+        def _():
+            load_weight()
+
         for h in range(2):
-            @pl.when(at_even(i, 16 + 8 * h))
+            @pl.when(at_even(i, V_AT[h]))
             def _():
-                spread_v(h, lax.div(i - 16 - 8 * h, 2))
+                spread_v(h, lax.div(i - V_AT[h], 2))
 
         @pl.when(at(i, LAG, 16 + LAG))
         def _():
             relay_k(i - LAG)
 
         for h in range(2):
-            @pl.when(at_even(i, 16 + 8 * h + LAG))
+            @pl.when(at_even(i, V_AT[h] + V_LAG))
             def _():
-                relay_v(h, lax.div(i - 16 - 8 * h - LAG, 2))
+                relay_v(h, lax.div(i - V_AT[h] - V_LAG, 2))
 
         @pl.when(at(i, LAG_FAR, 16 + LAG_FAR))
         def _():
             last_k(i - LAG_FAR)
 
         for h in range(2):
-            @pl.when(at_even(i, 16 + 8 * h + LAG_FAR))
+            @pl.when(at_even(i, V_AT[h] + V_FAR))
             def _():
-                last_v(h, lax.div(i - 16 - 8 * h - LAG_FAR, 2))
+                last_v(h, lax.div(i - V_AT[h] - V_FAR, 2))
 
         @pl.when(i == WEIGH_AT - 1)
         def _():
+            own[2].wait()
             arrived(qb.at[shares(0, 15)], q_recv)
             for plane in range(4):
                 arrived(kb.at[span], sib_recv.at[0, plane])
@@ -362,11 +385,12 @@
 
 def shards(queries, keys, values, rand_blocks, out_weight):
     any_spec = pl.BlockSpec(memory_space=pl.ANY)
+    hbm = pl.BlockSpec(memory_space=pltpu.HBM)
     dma = pltpu.SemaphoreType.DMA
     return pl.pallas_call(
         kernel,
         out_shape=jax.ShapeDtypeStruct((SHARE, D), jnp.bfloat16),
-        in_specs=[pl.BlockSpec(memory_space=pltpu.SMEM)] + [any_spec] * 4,
+        in_specs=[pl.BlockSpec(memory_space=pltpu.SMEM)] + [hbm] * 4,
         out_specs=any_spec,
         scratch_shapes=[
             pltpu.VMEM((NB, BLK, DH), jnp.bfloat16),
@@ -386,7 +410,7 @@
         ],
         compiler_params=pltpu.CompilerParams(
             collective_id=0, has_side_effects=True, vmem_limit_bytes=VMEM_MIB * 1024 * 1024),
-    )(rand_blocks.T, queries, keys.reshape(4, BLK, H * DH), values, out_weight)
+    )(rand_blocks.T, *[pltpu.with_memory_space_constraint(a, pltpu.HBM) for a in (queries, keys.reshape(4, BLK, H * DH), values, out_weight)])
 
 
 def solution(mesh):

time: 106 us -> 101 us (0.953)
  local copies, waits for them, and re-layouts: 5.69 us -> 2.02 us
    unnamed x9 -> x3, local copies, waits for them, and re-layouts: 5.69 us -> 2.02 us
    pallas_call x1, Pallas kernels: 100 us -> 99.1 us  [shards(): pl.pallas_call(kernel, out_shape=jax.ShapeDtypeStruct((SHARE, D), jnp.bfl...]
where the time goes in v4:
time: 101 us
  Pallas kernels  99.1 us (98%)
  local copies, waits for them, and re-layouts  2.02 us (2%)
    pallas_call x1, Pallas kernels, shards(): pl.pallas_call(kernel, out_shape=jax.ShapeDtypeStruct((SHARE, D), jnp.bfl...  99.1 us

profile of v4, /device:TPU:1, one launch (start us, length us, event | category | flops | bytes accessed | tf_op | source)
XLA Modules:
  0.0 101.1 jit_solution(16673608061207705794)
XLA Ops:
  0.0 0.0 copy-start
  0.0 0.7 copy-done
  0.7 99.1 %shard_map.55 = bf16[256,4096]{1,0:T(8,128)(2,1)S(1)} custom-call(s32[3,512]{1,0:T(4,128)S(1)} %bitcast.2, bf16[256,2048]{1,0:T(8,128)(2,1)} %q_in.1, bf16[4,64,2048]{2,1,0:T(8,128)(2,1)} %bitcast.3, bf16[256,2048]{1,0:T(8,128)(2,1)} %v_in.1, bf16[2048,4096]{1,0:T(8,128)(2,1)} %w_in.1), custom_call_target="tpu_custom_call" | custom-call | tf_op jit(solution)/shard_map/pallas_call | solution.py:390
  99.8 1.3 %copy.7 = bf16[256,4096]{1,0:T(8,128)(2,1)} copy(bf16[256,4096]{1,0:T(8,128)(2,1)S(1)} %shard_map.55) | data formatting | bytes 4194304
Async XLA Ops:
  0.0 0.7 copy-start

commit v5 on v4

--- a/solution.py
+++ b/solution.py
@@ -44,7 +44,7 @@
 def kernel(rand, q_in, k_in, v_in, w_in, out,
            kb, vb0, vb1, qb, pb, va, vp, ob, att, wv, acc,
            own_sem, s1_send, k_recv, v_recv, q_recv, k_up, k_dn, k_far, v_up, v_dn, v_far,
-           ring_send, sib_send, sib_recv, ret_send, ret_recv, w_sem, out_sem):
+           ring_send, sib_send, sib_recv, ret_send, ret_recv, w_sem, out_sem, row_in):
     ctx, ulys = lax.axis_index("ctx"), lax.axis_index("ulys")
     core = lax.rem(ctx, 2)
     y = lax.rem(lax.div(ctx, 2), 4)
@@ -70,7 +70,7 @@
         return pl.ds(token_share(px, py, zz, core) * 4, 4)
 
     def rows_x(g, zz):
-        return pl.ds(token_share(0, lax.rem(y + g, 4), zz, core) * 4, 16)
+        return pl.ds(token_share(lax.rem(g, 2) * 2, lax.rem(y + lax.div(g, 2), 4), zz, core) * 4, 8)
 
     def shares(k, count=1):
         return pl.ds(pl.multiple_of(k * SHARE, SHARE), count * SHARE)
@@ -90,13 +90,13 @@
     barrier = pltpu.get_barrier_semaphore()
     for device in (up, dn, sib):
         pl.semaphore_signal(barrier, inc=1, device_id=device, device_id_type=MESH)
-
-    @pl.loop(1, 16)
-    def _(k):
+    for k in (1, 2, 3, 4, 8, 12):
         px, py = back(k)
         pl.semaphore_signal(barrier, inc=1, device_id=mesh_id(px, py, z, core), device_id_type=MESH)
-
-    pl.semaphore_wait(barrier, 18)
+    pl.semaphore_wait(barrier, 9)
+    for k in (4, 8, 12):
+        px, py = back(k)
+        pl.semaphore_signal(row_in, inc=1, device_id=mesh_id(px, py, z, core), device_id_type=MESH)
 
     def push(src, dst, send, recv, device):
         pltpu.make_async_remote_copy(
@@ -159,10 +159,17 @@
     own[0].wait()
     spread_k(0)
 
-    @pl.loop(1, 16)
-    def _(k):
+    def send_keys(k):
         px, py = back(k)
         push(k_in.at[:, :, lanes(py * 4 + px)], kb.at[my_rows], s1_send.at[0], k_recv.at[k], mesh_id(px, py, z, core))
+
+    for k in (1, 2, 3, 4, 8, 12):
+        send_keys(k)
+    pl.semaphore_wait(row_in, 3)
+
+    @pl.loop(0, 9)
+    def _(n):
+        send_keys(5 + lax.div(n, 3) * 4 + lax.rem(n, 3))
 
     def send_queries():
         @pl.loop(1, 16)
@@ -188,12 +195,12 @@
                 vp[1, h, blk] = jnp.where(low_half, swap(top), bottom).astype(jnp.bfloat16)
 
         for h in range(2):
-            pltpu.make_async_copy(vp.at[h, head], vbs[h].at[my_rows], v_recv.at[h, 0]).start()
+            pltpu.make_async_copy(vp.at[h, head], vbs[h].at[my_rows], v_recv.at[h, lax.div(x, 2)]).start()
 
             @pl.loop(1, 16)
             def _(k):
                 px, py = back(k)
-                push(vp.at[h, py * 4 + px], vbs[h].at[my_rows], s1_send.at[2 + h], v_recv.at[h, lax.div(k, 4)],
+                push(vp.at[h, py * 4 + px], vbs[h].at[my_rows], s1_send.at[2 + h], v_recv.at[h, lax.div(k, 4) * 2 + lax.div(x, 2)],
                      mesh_id(px, py, z, core))
 
     def load_weight():
@@ -266,8 +273,8 @@
     def at(i, begin, end):
         return (i >= begin) & (i < end)
 
-    def at_even(i, begin):
-        return (i >= begin) & (i < begin + 8) & (lax.rem(i - begin, 2) == 0)
+    def at_eight(i, begin):
+        return (i >= begin) & (i < begin + 8)
 
     @pl.loop(1, STOP)
     def _(i):
@@ -289,27 +296,27 @@
             load_weight()
 
         for h in range(2):
-            @pl.when(at_even(i, V_AT[h]))
+            @pl.when(at_eight(i, V_AT[h]))
             def _():
-                spread_v(h, lax.div(i - V_AT[h], 2))
+                spread_v(h, i - V_AT[h])
 
         @pl.when(at(i, LAG, 16 + LAG))
         def _():
             relay_k(i - LAG)
 
         for h in range(2):
-            @pl.when(at_even(i, V_AT[h] + V_LAG))
+            @pl.when(at_eight(i, V_AT[h] + V_LAG))
             def _():
-                relay_v(h, lax.div(i - V_AT[h] - V_LAG, 2))
+                relay_v(h, i - V_AT[h] - V_LAG)
 
         @pl.when(at(i, LAG_FAR, 16 + LAG_FAR))
         def _():
             last_k(i - LAG_FAR)
 
         for h in range(2):
-            @pl.when(at_even(i, V_AT[h] + V_FAR))
+            @pl.when(at_eight(i, V_AT[h] + V_FAR))
             def _():
-                last_v(h, lax.div(i - V_AT[h] - V_FAR, 2))
+                last_v(h, i - V_AT[h] - V_FAR)
 
         @pl.when(i == WEIGH_AT - 1)
         def _():
@@ -404,9 +411,9 @@
             pltpu.VMEM((2, SHARE // 2, H * DH), jnp.bfloat16),
             pltpu.VMEM((2, H * DH // 2, D), jnp.bfloat16),
             pltpu.VMEM((SHARE, D), jnp.float32),
-            dma((3,)), dma((4,)), dma((16,)), dma((2, 4)), dma,
-            dma((16,)), dma((16,)), dma((16,)), dma((2, 4)), dma((2, 4)), dma((2, 4)),
-            dma((3, 4)), dma((3, 4)), dma((3, 4)), dma((2,)), dma((2,)), dma((2,)), dma,
+            dma((3,)), dma((4,)), dma((16,)), dma((2, 8)), dma,
+            dma((16,)), dma((16,)), dma((16,)), dma((2, 8)), dma((2, 8)), dma((2, 8)),
+            dma((3, 4)), dma((3, 4)), dma((3, 4)), dma((2,)), dma((2,)), dma((2,)), dma, pltpu.SemaphoreType.REGULAR,
         ],
         compiler_params=pltpu.CompilerParams(
             collective_id=0, has_side_effects=True, vmem_limit_bytes=VMEM_MIB * 1024 * 1024),

time: 101 us -> 99.2 us (0.982)
  Pallas kernels: 99.1 us -> 97 us
    pallas_call x1, Pallas kernels: 99.1 us -> 97 us  [shards(): pl.pallas_call(kernel, out_shape=jax.ShapeDtypeStruct((SHARE, D), jnp.bfl...]
where the time goes in v5:
time: 99.2 us; the launch traced here: 99 us
  Pallas kernels  97 us (98%)
  local copies, waits for them, and re-layouts  2.02 us (2%)
    pallas_call x1, Pallas kernels, shards(): pl.pallas_call(kernel, out_shape=jax.ShapeDtypeStruct((SHARE, D), jnp.bfl...  97 us
    unnamed x3, local copies, waits for them, and re-layouts  2.02 us

profile of v5, /device:TPU:1, one launch (start us, length us, event | category | flops | bytes accessed | tf_op | source)
XLA Modules:
  0.0 99.0 jit_solution(10384060596726262721)
XLA Ops:
  0.0 0.0 copy-start
  0.0 0.7 copy-done
  0.7 97.0 %shard_map.55 = bf16[256,4096]{1,0:T(8,128)(2,1)S(1)} custom-call(s32[3,512]{1,0:T(4,128)S(1)} %bitcast.2, bf16[256,2048]{1,0:T(8,128)(2,1)} %q_in.1, bf16[4,64,2048]{2,1,0:T(8,128)(2,1)} %bitcast.3, bf16[256,2048]{1,0:T(8,128)(2,1)} %v_in.1, bf16[2048,4096]{1,0:T(8,128)(2,1)} %w_in.1), custom_call_target="tpu_custom_call" | custom-call | tf_op jit(solution)/shard_map/pallas_call | solution.py:397
  97.7 1.3 %copy.7 = bf16[256,4096]{1,0:T(8,128)(2,1)} copy(bf16[256,4096]{1,0:T(8,128)(2,1)S(1)} %shard_map.55) | data formatting | bytes 4194304
Async XLA Ops:
  0.0 0.7 copy-start

commit v6 on v5

--- a/solution.py
+++ b/solution.py
@@ -16,15 +16,15 @@
 SHARE = 256
 MESH = pl.DeviceIdType.MESH
 TILE_N = 512
-LAG = 6
-LAG_FAR = 12
+LAG = 4
+LAG_FAR = 9
 V_AT = (16, 26)
 V_LAG = 4
 V_FAR = 8
 Q_AT = 4
 PACK_AT = 6
 W_AT = 10
-WEIGH_AT = 28
+WEIGH_AT = 25
 FIRST_AT = 32
 STOP = 42
 VMEM_MIB = 47
@@ -41,10 +41,10 @@
     return ctx * 8 + ulys
 
 
-def kernel(rand, q_in, k_in, v_in, w_in, out,
+def kernel(rand_in, q_in, k_in, v_in, w_in, out,
            kb, vb0, vb1, qb, pb, va, vp, ob, att, wv, acc,
            own_sem, s1_send, k_recv, v_recv, q_recv, k_up, k_dn, k_far, v_up, v_dn, v_far,
-           ring_send, sib_send, sib_recv, ret_send, ret_recv, w_sem, out_sem, row_in):
+           ring_send, sib_send, sib_recv, ret_send, ret_recv, w_sem, out_sem, row_in, rand):
     ctx, ulys = lax.axis_index("ctx"), lax.axis_index("ulys")
     core = lax.rem(ctx, 2)
     y = lax.rem(lax.div(ctx, 2), 4)
@@ -80,6 +80,7 @@
 
     my_rows = rows(0, z)
     own = [
+        pltpu.make_async_copy(rand_in, rand, own_sem.at[3]),
         pltpu.make_async_copy(k_in.at[:, :, lanes(head)], kb.at[my_rows], own_sem.at[0]),
         pltpu.make_async_copy(v_in, va, own_sem.at[1]),
         pltpu.make_async_copy(q_in.at[:, lanes(head)], qb.at[shares(0)], own_sem.at[2]),
@@ -156,7 +157,7 @@
         arrived(piece, v_far.at[h, g])
         share_on(1 + h, piece, 3)
 
-    own[0].wait()
+    own[1].wait()
     spread_k(0)
 
     def send_keys(k):
@@ -184,7 +185,7 @@
         return pltpu.roll(a, DH // 2, axis=1)
 
     def send_values():
-        own[1].wait()
+        own[2].wait()
 
         @pl.loop(0, 16)
         def _(h):
@@ -261,7 +262,7 @@
 
             @pl.when(k > 0)
             def _():
-                push(ob.at[h, packed(k)], att.at[h, :, lanes(k)], ret_send.at[h], ret_recv.at[h], mesh_id(px, py, z, core))
+                push(ob.at[h, packed(k)], att.at[h, :, lanes(k)], ret_send.at[h], ret_recv.at[h + h * lax.div(k, 8)], mesh_id(px, py, z, core))
 
             @pl.when(k == 0)
             def _():
@@ -320,7 +321,8 @@
 
         @pl.when(i == WEIGH_AT - 1)
         def _():
-            own[2].wait()
+            own[0].wait()
+            own[3].wait()
             arrived(qb.at[shares(0, 15)], q_recv)
             for plane in range(4):
                 arrived(kb.at[span], sib_recv.at[0, plane])
@@ -345,8 +347,8 @@
     def _(g):
         attend(1, g)
 
-    def unpack(h):
-        for pair in range(8):
+    def unpack(h, begin, end):
+        for pair in range(begin, end):
             a = att[h, :, 2 * pair * DH:(2 * pair + 1) * DH].astype(jnp.float32)
             b = att[h, :, (2 * pair + 1) * DH:(2 * pair + 2) * DH].astype(jnp.float32)
             cols = slice(h * 1024 + pair * DH, h * 1024 + (pair + 1) * DH)
@@ -358,19 +360,26 @@
 
     arrived(wv.at[0], w_sem.at[0])
     arrived(ob.at[0], ret_recv.at[0])
-    unpack(0)
+    unpack(0, 0, 8)
 
     @pl.loop(0, D // TILE_N)
     def _(n):
         acc[:, tile(n)] = jnp.dot(va[:, 0:1024], wv[0, :, tile(n)], preferred_element_type=jnp.float32)
 
     arrived(wv.at[1], w_sem.at[1])
-    arrived(ob.at[1], ret_recv.at[1])
-    unpack(1)
+    arrived(ob.at[1, packed(0, 8)], ret_recv.at[1])
+    unpack(1, 0, 4)
 
     @pl.loop(0, D // TILE_N)
     def _(n):
-        total = acc[:, tile(n)] + jnp.dot(va[:, 1024:2048], wv[1, :, tile(n)], preferred_element_type=jnp.float32)
+        acc[:, tile(n)] += jnp.dot(va[:, 1024:1536], wv[1, 0:512, tile(n)], preferred_element_type=jnp.float32)
+
+    arrived(ob.at[1, packed(0, 8)], ret_recv.at[2])
+    unpack(1, 4, 8)
+
+    @pl.loop(0, D // TILE_N)
+    def _(n):
+        total = acc[:, tile(n)] + jnp.dot(va[:, 1536:2048], wv[1, 512:1024, tile(n)], preferred_element_type=jnp.float32)
         total = total.astype(jnp.bfloat16)
         done = jnp.concatenate([total[0:64], total[128:192], total[64:128], total[192:256]], axis=0)
         pb[shares(n), :] = done
@@ -397,7 +406,7 @@
     return pl.pallas_call(
         kernel,
         out_shape=jax.ShapeDtypeStruct((SHARE, D), jnp.bfloat16),
-        in_specs=[pl.BlockSpec(memory_space=pltpu.SMEM)] + [hbm] * 4,
+        in_specs=[hbm] * 5,
         out_specs=any_spec,
         scratch_shapes=[
             pltpu.VMEM((NB, BLK, DH), jnp.bfloat16),
@@ -411,13 +420,14 @@
             pltpu.VMEM((2, SHARE // 2, H * DH), jnp.bfloat16),
             pltpu.VMEM((2, H * DH // 2, D), jnp.bfloat16),
             pltpu.VMEM((SHARE, D), jnp.float32),
-            dma((3,)), dma((4,)), dma((16,)), dma((2, 8)), dma,
+            dma((4,)), dma((4,)), dma((16,)), dma((2, 8)), dma,
             dma((16,)), dma((16,)), dma((16,)), dma((2, 8)), dma((2, 8)), dma((2, 8)),
-            dma((3, 4)), dma((3, 4)), dma((3, 4)), dma((2,)), dma((2,)), dma((2,)), dma, pltpu.SemaphoreType.REGULAR,
+            dma((3, 4)), dma((3, 4)), dma((3, 4)), dma((2,)), dma((3,)), dma((2,)), dma, pltpu.SemaphoreType.REGULAR,
+            pltpu.SMEM((3, NB), jnp.int32),
         ],
         compiler_params=pltpu.CompilerParams(
             collective_id=0, has_side_effects=True, vmem_limit_bytes=VMEM_MIB * 1024 * 1024),
-    )(rand_blocks.T, *[pltpu.with_memory_space_constraint(a, pltpu.HBM) for a in (queries, keys.reshape(4, BLK, H * DH), values, out_weight)])
+    )(*[pltpu.with_memory_space_constraint(a, pltpu.HBM) for a in (rand_blocks.T, queries, keys.reshape(4, BLK, H * DH), values, out_weight)])
 
 
 def solution(mesh):

time: 99.2 us -> 97.2 us (0.980)
  Pallas kernels: 97 us -> 95.8 us
    pallas_call x1, Pallas kernels: 97 us -> 95.8 us  [shards(): pl.pallas_call(kernel, out_shape=jax.ShapeDtypeStruct((SHARE, D), jnp.bfl...]
    unnamed x3 -> x1, local copies, waits for them, and re-layouts: 2.02 us -> 1.32 us
where the time goes in v6:
time: 97.2 us; the launch traced here: 97.1 us
  Pallas kernels  95.8 us (99%)
  local copies, waits for them, and re-layouts  1.32 us (1%)
    pallas_call x1, Pallas kernels, shards(): pl.pallas_call(kernel, out_shape=jax.ShapeDtypeStruct((SHARE, D), jnp.bfl...  95.8 us

profile of v6, /device:TPU:1, one launch (start us, length us, event | category | flops | bytes accessed | tf_op | source)
XLA Modules:
  0.0 97.1 jit_solution(16828229049570044537)
XLA Ops:
  0.0 95.8 %shard_map.55 = bf16[256,4096]{1,0:T(8,128)(2,1)S(1)} custom-call(s32[3,512]{1,0:T(4,128)} %bitcast.3, bf16[256,2048]{1,0:T(8,128)(2,1)} %q_in.1, bf16[4,64,2048]{2,1,0:T(8,128)(2,1)} %bitcast.2, bf16[256,2048]{1,0:T(8,128)(2,1)} %v_in.1, bf16[2048,4096]{1,0:T(8,128)(2,1)} %w_in.1), custom_call_target="tpu_custom_call" | custom-call | tf_op jit(solution)/shard_map/pallas_call | solution.py:406
  95.8 1.3 %copy.7 = bf16[256,4096]{1,0:T(8,128)(2,1)} copy(bf16[256,4096]{1,0:T(8,128)(2,1)S(1)} %shard_map.55) | data formatting | bytes 4194304

commit v7 on v6

--- a/solution.py
+++ b/solution.py
@@ -18,7 +18,7 @@
 TILE_N = 512
 LAG = 4
 LAG_FAR = 9
-V_AT = (16, 26)
+V_AT = (16, 27)
 V_LAG = 4
 V_FAR = 8
 Q_AT = 4
@@ -26,7 +26,8 @@
 W_AT = 10
 WEIGH_AT = 25
 FIRST_AT = 32
-STOP = 42
+PART = 8
+STOP = 43
 VMEM_MIB = 47
 GANG = 2
 EXP_SCALE = (DH ** -0.5) * 1.4426950408889634
@@ -85,15 +86,14 @@
         pltpu.make_async_copy(v_in, va, own_sem.at[1]),
         pltpu.make_async_copy(q_in.at[:, lanes(head)], qb.at[shares(0)], own_sem.at[2]),
     ]
-    for copy in own:
-        copy.start()
-
     barrier = pltpu.get_barrier_semaphore()
     for device in (up, dn, sib):
         pl.semaphore_signal(barrier, inc=1, device_id=device, device_id_type=MESH)
     for k in (1, 2, 3, 4, 8, 12):
         px, py = back(k)
         pl.semaphore_signal(barrier, inc=1, device_id=mesh_id(px, py, z, core), device_id_type=MESH)
+    for copy in own:
+        copy.start()
     pl.semaphore_wait(barrier, 9)
     for k in (4, 8, 12):
         px, py = back(k)
@@ -262,7 +262,7 @@
 
             @pl.when(k > 0)
             def _():
-                push(ob.at[h, packed(k)], att.at[h, :, lanes(k)], ret_send.at[h], ret_recv.at[h + h * lax.div(k, 8)], mesh_id(px, py, z, core))
+                push(ob.at[h, packed(k)], att.at[h, :, lanes(k)], ret_send.at[h], ret_recv.at[h + h * lax.div(k, PART)], mesh_id(px, py, z, core))
 
             @pl.when(k == 0)
             def _():
@@ -367,19 +367,19 @@
         acc[:, tile(n)] = jnp.dot(va[:, 0:1024], wv[0, :, tile(n)], preferred_element_type=jnp.float32)
 
     arrived(wv.at[1], w_sem.at[1])
-    arrived(ob.at[1, packed(0, 8)], ret_recv.at[1])
-    unpack(1, 0, 4)
+    arrived(ob.at[1, packed(0, PART)], ret_recv.at[1])
+    unpack(1, 0, PART // 2)
 
     @pl.loop(0, D // TILE_N)
     def _(n):
-        acc[:, tile(n)] += jnp.dot(va[:, 1024:1536], wv[1, 0:512, tile(n)], preferred_element_type=jnp.float32)
-
-    arrived(ob.at[1, packed(0, 8)], ret_recv.at[2])
-    unpack(1, 4, 8)
+        acc[:, tile(n)] += jnp.dot(va[:, 1024:1024 + PART * 64], wv[1, 0:PART * 64, tile(n)], preferred_element_type=jnp.float32)
+
+    arrived(ob.at[1, packed(0, 16 - PART)], ret_recv.at[2])
+    unpack(1, PART // 2, 8)
 
     @pl.loop(0, D // TILE_N)
     def _(n):
-        total = acc[:, tile(n)] + jnp.dot(va[:, 1536:2048], wv[1, 512:1024, tile(n)], preferred_element_type=jnp.float32)
+        total = acc[:, tile(n)] + jnp.dot(va[:, 1024 + PART * 64:2048], wv[1, PART * 64:1024, tile(n)], preferred_element_type=jnp.float32)
         total = total.astype(jnp.bfloat16)
         done = jnp.concatenate([total[0:64], total[128:192], total[64:128], total[192:256]], axis=0)
         pb[shares(n), :] = done

time: 97.2 us -> 97.1 us (level)
  no operation moved by 1% of the time
where the time goes in v7:
time: 97.1 us; the launch traced here: 97 us
  Pallas kernels  95.7 us (99%)
  local copies, waits for them, and re-layouts  1.32 us (1%)
    pallas_call x1, Pallas kernels, shards(): pl.pallas_call(kernel, out_shape=jax.ShapeDtypeStruct((SHARE, D), jnp.bfl...  95.7 us

profile of v7, /device:TPU:1, one launch (start us, length us, event | category | flops | bytes accessed | tf_op | source)
XLA Modules:
  0.0 97.0 jit_solution(9971817252064684802)
XLA Ops:
  0.0 95.7 %shard_map.55 = bf16[256,4096]{1,0:T(8,128)(2,1)S(1)} custom-call(s32[3,512]{1,0:T(4,128)} %bitcast.3, bf16[256,2048]{1,0:T(8,128)(2,1)} %q_in.1, bf16[4,64,2048]{2,1,0:T(8,128)(2,1)} %bitcast.2, bf16[256,2048]{1,0:T(8,128)(2,1)} %v_in.1, bf16[2048,4096]{1,0:T(8,128)(2,1)} %w_in.1), custom_call_target="tpu_custom_call" | custom-call | tf_op jit(solution)/shard_map/pallas_call | solution.py:406
  95.7 1.3 %copy.7 = bf16[256,4096]{1,0:T(8,128)(2,1)} copy(bf16[256,4096]{1,0:T(8,128)(2,1)S(1)} %shard_map.55) | data formatting | bytes 4194304

commit v8 on v7

--- a/solution.py
+++ b/solution.py
@@ -26,7 +26,7 @@
 W_AT = 10
 WEIGH_AT = 25
 FIRST_AT = 32
-PART = 8
+PART = 6
 STOP = 43
 VMEM_MIB = 47
 GANG = 2
@@ -262,7 +262,7 @@
 
             @pl.when(k > 0)
             def _():
-                push(ob.at[h, packed(k)], att.at[h, :, lanes(k)], ret_send.at[h], ret_recv.at[h + h * lax.div(k, PART)], mesh_id(px, py, z, core))
+                push(ob.at[h, packed(k)], att.at[h, :, lanes(k)], ret_send.at[h], ret_recv.at[h + h * lax.min(lax.div(k, PART), 1)], mesh_id(px, py, z, core))
 
             @pl.when(k == 0)
             def _():

time: 97.1 us -> 96.8 us (level)
  no operation moved by 1% of the time
where the time goes in v8:
time: 96.8 us; the launch traced here: 96.7 us
  Pallas kernels  95.4 us (99%)
  local copies, waits for them, and re-layouts  1.32 us (1%)
    pallas_call x1, Pallas kernels, shards(): pl.pallas_call(kernel, out_shape=jax.ShapeDtypeStruct((SHARE, D), jnp.bfl...  95.4 us

profile of v8, /device:TPU:1, one launch (start us, length us, event | category | flops | bytes accessed | tf_op | source)
XLA Modules:
  0.0 96.7 jit_solution(7584620139034966942)
XLA Ops:
  0.0 95.4 %shard_map.55 = bf16[256,4096]{1,0:T(8,128)(2,1)S(1)} custom-call(s32[3,512]{1,0:T(4,128)} %bitcast.3, bf16[256,2048]{1,0:T(8,128)(2,1)} %q_in.1, bf16[4,64,2048]{2,1,0:T(8,128)(2,1)} %bitcast.2, bf16[256,2048]{1,0:T(8,128)(2,1)} %v_in.1, bf16[2048,4096]{1,0:T(8,128)(2,1)} %w_in.1), custom_call_target="tpu_custom_call" | custom-call | tf_op jit(solution)/shard_map/pallas_call | solution.py:406
  95.4 1.3 %copy.7 = bf16[256,4096]{1,0:T(8,128)(2,1)} copy(bf16[256,4096]{1,0:T(8,128)(2,1)S(1)} %shard_map.55) | data formatting | bytes 4194304

commit v9 on v8

--- a/solution.py
+++ b/solution.py
@@ -26,7 +26,7 @@
 W_AT = 10
 WEIGH_AT = 25
 FIRST_AT = 32
-PART = 6
+PART = 4
 STOP = 43
 VMEM_MIB = 47
 GANG = 2

time: 96.8 us -> 96.8 us (level)
  no operation moved by 1% of the time
where the time goes in v9:
time: 96.8 us; the launch traced here: 96.7 us
  Pallas kernels  95.3 us (98%)
  local copies, waits for them, and re-layouts  1.32 us (1%)
    pallas_call x1, Pallas kernels, shards(): pl.pallas_call(kernel, out_shape=jax.ShapeDtypeStruct((SHARE, D), jnp.bfl...  95.3 us

profile of v9, /device:TPU:1, one launch (start us, length us, event | category | flops | bytes accessed | tf_op | source)
XLA Modules:
  0.0 96.7 jit_solution(8197700296393972051)
XLA Ops:
  0.0 95.3 %shard_map.55 = bf16[256,4096]{1,0:T(8,128)(2,1)S(1)} custom-call(s32[3,512]{1,0:T(4,128)} %bitcast.3, bf16[256,2048]{1,0:T(8,128)(2,1)} %q_in.1, bf16[4,64,2048]{2,1,0:T(8,128)(2,1)} %bitcast.2, bf16[256,2048]{1,0:T(8,128)(2,1)} %v_in.1, bf16[2048,4096]{1,0:T(8,128)(2,1)} %w_in.1), custom_call_target="tpu_custom_call" | custom-call | tf_op jit(solution)/shard_map/pallas_call | solution.py:406
  95.3 1.3 %copy.7 = bf16[256,4096]{1,0:T(8,128)(2,1)} copy(bf16[256,4096]{1,0:T(8,128)(2,1)S(1)} %shard_map.55) | data formatting | bytes 4194304
